TPU v7x, 32 devices: a whole 2x2x4 slice. The times are simulated.
32 devices in a mesh: groups: 2 (over x), rows: 8 (over z, y), chan: 2 (over core).
Axes of the slice: x: 2, y: 2, z: 4, core: 2. Of those that a mesh axis runs over, the one named last changes fastest.
Arguments:
- latents: bfloat16 [48, 32, 1024], P('groups', 'rows', 'chan'), parts along dimension 0, may hold values from -6 to 6
- timestep: int32 [6], P('groups'), parts along dimension 0, may hold values from 0 to 999
- label: int32 [6], P('groups'), parts along dimension 0, may hold values from 0 to 15
- time_table: bfloat16 [1000, 1024], P(None, 'chan'), may hold values from -3 to 3
- class_table: bfloat16 [16, 1024], replicated, may hold values from -6 to 6
- dw_kernel: bfloat16 [7, 7, 1024], P(None, None, 'chan'), may hold values from -0.875 to 0.875
- dw_bias: bfloat16 [1024], P('chan'), may hold values from -3 to 3
- ln_gain: bfloat16 [1024], P('chan'), may hold values from 0.25 to 1.75
- ln_bias: bfloat16 [1024], P('chan'), may hold values from -2 to 2
- up_weight: bfloat16 [1024, 4096], P(None, 'chan'), may hold values from -0.1875 to 0.1875
- up_bias: bfloat16 [4096], P('chan'), may hold values from -3 to 3
- down_weight: bfloat16 [4096, 1024], P('chan'), may hold values from -0.09375 to 0.09375
- down_bias: bfloat16 [1024], P('chan'), may hold values from -3 to 3
- layer_scale: bfloat16 [1024], replicated, may hold values from 0.5 to 1.5
Outputs:
- features: bfloat16 [48, 32, 1024], P(('groups', 'rows'), None, 'chan'), parts along dimension 0
- gradient: float32 [48, 32, 1024], P('groups', 'rows', 'chan'), parts along dimension 0
There are 2 independent parts, one for each index of `groups`. A program takes and returns all parts, laid end to end along the dimension named above; an argument that names none is the same for every part. Nothing has to cross between parts.
Inputs may be any that keep to these rules, and one draw needn't show every extreme that they name: One timestep index for each image, a row of the table of 1000 timesteps. `label`: one defect class for each image, out of 16 classes.
All inputs are finite; a program needn't handle non-finite values.
Results may differ from a plain program's by a relative error of at most 0.0045.
Values may be sent and summed in bfloat16 or wider, within the bound.
No kernel may reach another device: no remote copies, remote signals or barrier semaphores. Data moves between devices by JAX's collectives and lax.ppermute only.
A program may use at most 128 MiB of HBM per device.

v0:
```python
import jax
import jax.numpy as jnp
from jax import lax
from jax.sharding import PartitionSpec as P

KAPPA = 0.7978845608028654
EPSILON = 1e-06


def with_halo(cells, sides, width):
    for axis, dim in sides:
        count = lax.axis_size(axis)
        ends = count - 1
        head = lax.slice_in_dim(cells, 0, width, axis=dim)
        tail = lax.slice_in_dim(cells, cells.shape[dim] - width, cells.shape[dim], axis=dim)
        cells = jnp.concatenate(
            [
                lax.ppermute(tail, axis, [(i, (i + 1) % count) for i in range(ends)]),
                cells,
                lax.ppermute(head, axis, [((i + 1) % count, i) for i in range(ends)]),
            ],
            axis=dim,
        )
    return cells


def gelu_tanh(values):
    inner = KAPPA * (values + 0.044715 * values * values * values)
    return 0.5 * values * (1.0 + jnp.tanh(inner))


def gelu_slope(values):
    tangent = jnp.tanh(KAPPA * (values + 0.044715 * values * values * values))
    return 0.5 * (1.0 + tangent) + 0.5 * values * (1.0 - tangent * tangent) * KAPPA * (
        1.0 + 3.0 * 0.044715 * values * values
    )


def stencil(padded, kernel, masks):
    height = padded.shape[0] - 6
    width = padded.shape[1] - 6
    total = jnp.zeros((height, width, padded.shape[2]), jnp.float32)
    for row_tap in range(7):
        partial_row = jnp.zeros((height, width, padded.shape[2]), jnp.float32)
        for col_tap in range(7):
            partial_row = (
                partial_row
                + padded[row_tap : row_tap + height, col_tap : col_tap + width, :]
                * kernel[row_tap, col_tap]
            )
        total = total + partial_row * masks[row_tap][:, None, None]
    return total


def exact_dot(left, right):
    return jnp.dot(left, right, precision=lax.Precision.HIGHEST, preferred_element_type=jnp.float32)


def local_block(
    latent_pad,
    row_first,
    col_first,
    total_rows,
    total_cols,
    pad_grad,
    time_rows,
    class_half,
    slope_image,
    scale_half,
    dw_kernel,
    dw_bias,
    ln_gain,
    ln_bias,
    up_weight,
    up_bias,
    down_weight,
    down_bias,
    full_channels,
):
    pad_rows = latent_pad.shape[0]
    pad_cols = latent_pad.shape[1]
    height = pad_rows - 6
    width = pad_cols - 6
    channels = latent_pad.shape[2]
    images = time_rows.shape[0]
    image_height = total_rows // images
    row_global = row_first - 3 + jnp.arange(pad_rows, dtype=jnp.int32)
    row_image = jnp.floor_divide(row_global, image_height)
    col_global = col_first - 3 + jnp.arange(pad_cols, dtype=jnp.int32)
    col_valid = ((col_global >= 0) & (col_global < total_cols)).astype(jnp.float32)
    image_hot = (row_image[:, None] == jnp.arange(images, dtype=jnp.int32)[None, :]).astype(
        jnp.float32
    )
    time_pad = exact_dot(image_hot, time_rows)
    start_pad = latent_pad.astype(jnp.float32) + time_pad[:, None, :] * col_valid[None, :, None]
    masks = jnp.stack(
        [
            (row_image[tap : tap + height] == row_image[3 : 3 + height]).astype(jnp.float32)
            for tap in range(7)
        ]
    )
    kernel = dw_kernel.astype(jnp.float32)
    mixed = stencil(start_pad, kernel, masks) + dw_bias.astype(jnp.float32)
    tokens = height * width
    flat = mixed.reshape(tokens, channels)
    first_sum, second_sum = lax.psum((jnp.sum(flat, 1), jnp.sum(flat * flat, 1)), "chan")
    mean = first_sum / full_channels
    variance = second_sum / full_channels - mean * mean
    inverse = lax.rsqrt(variance + EPSILON)
    normed = (flat - mean[:, None]) * inverse[:, None]
    gain = ln_gain.astype(jnp.float32)
    scaled = (normed * gain + ln_bias.astype(jnp.float32)).astype(jnp.bfloat16)
    hidden = jnp.dot(
        lax.all_gather(scaled, "chan", axis=1, tiled=True),
        up_weight,
        preferred_element_type=jnp.float32,
    )
    hidden = hidden + up_bias.astype(jnp.float32)
    active = gelu_tanh(hidden).astype(jnp.bfloat16)
    branch = lax.psum_scatter(
        jnp.dot(active, down_weight, preferred_element_type=jnp.float32),
        "chan",
        scatter_dimension=1,
        tiled=True,
    )
    branch = branch + down_bias.astype(jnp.float32)
    start_cells = start_pad[3 : 3 + height, 3 : 3 + width].reshape(tokens, channels)
    features = (
        (start_cells + scale_half * branch).astype(jnp.bfloat16).reshape(height, width, channels)
    )
    token_image = image_hot[3 : 3 + height]
    slope_rows = exact_dot(token_image, slope_image)
    slope_tokens = jnp.broadcast_to(
        slope_rows[:, None, :], (height, width, slope_rows.shape[1])
    ).reshape(tokens, slope_rows.shape[1])
    hidden_grad = (slope_tokens * gelu_slope(hidden)).astype(jnp.bfloat16)
    grad_terms = lax.dot_general(
        hidden_grad, up_weight, (((1,), (1,)), ((), ())), preferred_element_type=jnp.float32
    )
    normed_grad = lax.psum_scatter(
        grad_terms.astype(jnp.bfloat16), "chan", scatter_dimension=1, tiled=True
    ).astype(jnp.float32)
    gained = normed_grad * gain
    grad_first, grad_second = lax.psum((jnp.sum(gained, 1), jnp.sum(gained * normed, 1)), "chan")
    mixed_grad = inverse[:, None] * (
        gained - grad_first[:, None] / full_channels - normed * grad_second[:, None] / full_channels
    )
    grad_pad = pad_grad(mixed_grad.reshape(height, width, channels))
    class_tokens = exact_dot(token_image, class_half)
    gradient = stencil(grad_pad, kernel[::-1, ::-1], masks) + class_tokens[:, None, :]
    return (features, gradient)


def per_device(
    latents,
    timestep,
    label,
    time_table,
    class_table,
    dw_kernel,
    dw_bias,
    ln_gain,
    ln_bias,
    up_weight,
    up_bias,
    down_weight,
    down_bias,
    layer_scale,
):
    channels = ln_gain.shape[0]
    full_channels = class_table.shape[1]
    half_index = lax.axis_index("chan")
    scale_full = layer_scale.astype(jnp.float32)
    scale_half = lax.dynamic_slice_in_dim(scale_full, half_index * channels, channels, 0)
    time_hot = (
        timestep[:, None] == jnp.arange(time_table.shape[0], dtype=jnp.int32)[None, :]
    ).astype(jnp.float32)
    time_rows = exact_dot(time_hot, time_table.astype(jnp.float32))
    class_hot = (
        label[:, None] == jnp.arange(class_table.shape[0], dtype=jnp.int32)[None, :]
    ).astype(jnp.float32)
    class_rows = exact_dot(class_hot, class_table.astype(jnp.float32))
    class_half = lax.dynamic_slice_in_dim(class_rows, half_index * channels, channels, 1)
    direction = (class_rows * scale_full).astype(jnp.bfloat16)
    slope_image = lax.dot_general(
        direction, down_weight, (((1,), (1,)), ((), ())), preferred_element_type=jnp.float32
    )
    latent_rows = lax.all_to_all(latents, "rows", split_axis=0, concat_axis=1, tiled=True)
    height = latent_rows.shape[0]
    width = latent_rows.shape[1]
    row_first = lax.axis_index("rows") * height
    col_first = 0
    total_rows = height * lax.axis_size("rows")
    latent_pad = with_halo(latent_rows, (("rows", 0),), 3)
    latent_pad = jnp.pad(latent_pad, ((0, 0), (3, 3), (0, 0)))

    def pad_grad(field):
        padded = with_halo(field.astype(jnp.bfloat16), (("rows", 0),), 3).astype(field.dtype)
        return jnp.pad(padded, ((0, 0), (3, 3), (0, 0)))

    features, gradient = local_block(
        latent_pad,
        row_first,
        col_first,
        total_rows,
        width,
        pad_grad,
        time_rows,
        class_half,
        slope_image,
        scale_half,
        dw_kernel,
        dw_bias,
        ln_gain,
        ln_bias,
        up_weight,
        up_bias,
        down_weight,
        down_bias,
        full_channels,
    )
    gradient = lax.all_to_all(gradient, "rows", split_axis=1, concat_axis=0, tiled=True)
    return (features, gradient)


def solution(mesh):
    in_specs = (
        P("groups", "rows", "chan"),
        P("groups"),
        P("groups"),
        P(None, "chan"),
        P(),
        P(None, None, "chan"),
        P("chan"),
        P("chan"),
        P("chan"),
        P(None, "chan"),
        P("chan"),
        P("chan", None),
        P("chan"),
        P(),
    )
    out_specs = (P(("groups", "rows"), None, "chan"), P("groups", "rows", "chan"))
    return jax.shard_map(
        per_device, mesh=mesh, in_specs=in_specs, out_specs=out_specs, check_vma=False
    )
```

profile of v0, /device:TPU:0, one launch (start us, length us, event | category | flops | bytes accessed | tf_op | source)
XLA Modules:
  0.0 107.5 jit_solution(14234665979605698154)
XLA Ops:
  7.2 7.5 %all-to-all-start = ((bf16[24,4,512]{2,1,0:T(4,128)(2,1)}), bf16[24,4,512]{2,1,0:T(4,128)(2,1)S(1)}, u32[]{:S(2)}, u32[]{:S(2)}) async-start(bf16[24,4,512]{2,1,0:T(4,128)(2,1)} %param.14), calls=%async_computation | async-start | bytes 196608 | tf_op jit(solution)/shard_map/all_to_all | solution.py:188
  14.7 1.0 fusion.184
  15.8 1.1 %fusion.183 = (f32[1,1,512]{2,1,0:T(1,128)S(1)}, f32[1,1,512]{2,1,0:T(1,128)S(1)}, f32[1,1,512]{2,1,0:T(1,128)S(1)}, f32[1,1,512]{2,1,0:T(1,128)S(1)}, f32[1,1,5...) fusion(bf16[7,7,512]{2,1,0:T(8,128)(2,1)} %param.19), kind=kLoop, calls=%fused_computation.314 | loop fusion | bytes 77824 | tf_op jit(solution)/shard_map/slice | solution.py:49
  17.1 1.6 %fusion.182 = (f32[1,1,512]{2,1,0:T(1,128)S(1)}, f32[1,1,512]{2,1,0:T(1,128)S(1)}, f32[1,1,512]{2,1,0:T(1,128)S(1)}, f32[1,1,512]{2,1,0:T(1,128)S(1)}, f32[1,1,5...) fusion(bf16[7,7,512]{2,1,0:T(8,128)(2,1)} %param.19), kind=kLoop, calls=%fused_computation.313 | loop fusion | bytes 77824 | tf_op jit(solution)/shard_map/slice | solution.py:49
  18.9 0.7 convert_element_type.102
  19.6 0.7 convert_element_type.101
  21.0 0.7 convert_element_type.93
  21.7 0.7 convert_element_type.105
  22.4 0.9 fusion.163
  23.7 3.4 %fusion.164 = f32[3,2048]{1,0:T(4,128)S(1)} fusion(bf16[2048,1024]{1,0:T(8,128)(2,1)} %param.25, f32[3,1024]{1,0:T(4,128)S(1)} %fusion.169, f32[1024]{0:T(1024)S(1)} %convert_element_type.93), kind=kOutput, calls=%fused_computation.280 | convolution fusion | flops 12589056 | bytes 4235264 | tf_op jit(solution)/shard_map/dot_general | solution.py:185
  27.3 0.7 compare_convert_fusion.5
  28.0 1.3 %collective-permute-start.1 = (bf16[3,32,512]{2,0,1:T(4,128)(2,1)S(1)}, bf16[3,32,512]{2,0,1:T(4,128)(2,1)S(1)}, u32[]{:S(2)}, u32[]{:S(2)}) collective-permute-start(bf16[3,32,512]{2,0,1:T(4,128)(2,1)S(1)} %bitcast.86), channel_id=1, source_target_pairs={{2,0},{4,2},{6,4},{8,6},{10,8},{12,10},{14,12},{3,1},{5,3},{7,5},{... | collective-permute-start | bytes 294920 | tf_op jit(solution)/shard_map/ppermute | solution.py:20
  29.3 4.6 %collective-permute-start = (bf16[3,32,512]{2,0,1:T(4,128)(2,1)S(1)}, bf16[3,32,512]{2,0,1:T(4,128)(2,1)S(1)}, u32[]{:S(2)}, u32[]{:S(2)}) collective-permute-start(bf16[3,32,512]{2,0,1:T(4,128)(2,1)S(1)} %bitcast.87), channel_id=1, source_target_pairs={{0,2},{2,4},{4,6},{6,8},{8,10},{10,12},{12,14},{1,3},{3,5},{5,7},{... | collective-permute-start | bytes 294920 | tf_op jit(solution)/shard_map/ppermute | solution.py:18
  33.9 1.0 collective-permute-done.1
  34.9 2.9 %collective-permute-done = bf16[3,32,512]{2,0,1:T(4,128)(2,1)S(1)} collective-permute-done((bf16[3,32,512]{2,0,1:T(4,128)(2,1)S(1)}, bf16[3,32,512]{2,0,1:T(4,128)(2,1)S(1)}, u32[]{:S(2)}, u32[]{:S(2)}) %collective-permute-start) | collective-permute-done | bytes 98336 | tf_op jit(solution)/shard_map/ppermute | solution.py:18
  38.6 5.1 %fusion.180 = (f32[3,32]{0,1:T(8,128)S(1)}, f32[3,32]{0,1:T(8,128)S(1)}, f32[3,32,512]{2,0,1:T(4,128)S(1)}) fusion(f32[512]{0:T(512)S(1)} %convert_element_type.101, f32[3]{0:T(128)} %get-tuple-element.67, f32[512]{0:T(512)S(1)} %bitcast.113, f32[9,38,512]{2,0,1:T(8,128)S(1)} %multiply_add_fusion, f32[512]{0:T(512)S(1)} %bitcast.111, f32[512]{0:T(512)S(1)} %bitcast.109, ...), kind=kLoop, calls=%fused_computation.312 | loop fusion | flops 5259072 | bytes 9933640 | tf_op jit(solution)/shard_map/reduce_sum | solution.py:106
  44.0 2.5 %all-reduce.3 = (f32[96]{0:T(128)S(1)}, f32[96]{0:T(128)S(1)}) all-reduce(f32[96]{0:T(128)S(1)} %reduce_sum.43, f32[96]{0:T(128)S(1)} %reduce_sum.41), channel_id=1, replica_groups=mesh['groups'=2,'rows'=8,'chan'=2] {'chan'}, use_global_device_ids=true, to_apply=%region_3.4 | all-reduce | flops 192 | bytes 1536 | tf_op jit(solution)/shard_map/psum | solution.py:106
  46.6 1.9 %all_gather.3 = bf16[96,1024]{1,0:T(8,128)(2,1)S(1)} all-gather(bf16[96,512]{1,0:T(8,128)(2,1)S(1)} %add_convert_fusion), channel_id=1, replica_groups=mesh['groups'=2,'rows'=8,'chan'=2] {'chan'}, dimensions={1}, use_global_device_ids=true | all-gather | bytes 294912 | tf_op jit(solution)/shard_map/all_gather | solution.py:114
  48.6 3.6 %fusion.7 = (bf16[96,2048]{1,0:T(8,128)(2,1)S(1)}, f32[96,2048]{1,0:T(8,128)S(1)}) fusion(f32[3,2048]{1,0:T(4,128)S(1)} %fusion.171, f32[2048]{0:T(1024)S(1)} %convert_element_type.105, bf16[96,1024]{1,0:T(8,128)(2,1)S(1)} %all_gather.3, bf16[1024,2048]{1,0:T(8,128)(2,1)} %param.23), kind=kOutput, calls=%fused_computation.56 | convolution fusion | flops 406585344 | bytes 5603328 | tf_op jit(solution)/shard_map/dot_general | solution.py:113
  52.2 2.1 %convolution_convert_fusion = bf16[96,1024]{1,0:T(8,128)(2,1)} fusion(bf16[96,2048]{1,0:T(8,128)(2,1)S(1)} %get-tuple-element.68, bf16[1024,2048]{1,0:T(8,128)(2,1)S(1)} %copy-done.1), kind=kOutput, calls=%fused_computation.49 | convolution fusion | flops 402751488 | bytes 4784128 | tf_op jit(solution)/shard_map/dot_general | solution.py:137
  54.5 9.4 %reduce-scatter.5.cloned.1.call-done = bf16[96,512]{1,0:T(8,128)(2,1)} async-done(((bf16[96,1024]{1,0:T(8,128)(2,1)}), bf16[96,512]{1,0:T(8,128)(2,1)}) %reduce-scatter.5.cloned.1.call-update) | async-done | bytes 98320 | tf_op jit(solution)/shard_map/reduce_scatter | solution.py:140
  63.9 1.1 %fusion.162 = (f32[96]{0:T(128)S(1)}, f32[96]{0:T(128)S(1)}) fusion(bf16[96,512]{1,0:T(8,128)(2,1)} %reduce-scatter.5.cloned.1.call-done, f32[512]{0:T(512)S(1)} %convert_element_type.102, f32[96]{0:T(128)S(1)} %get-tuple-element.61, f32[96]{0:T(128)S(1)} %get-tuple-element.60, f32[3,32,512]{2,1,0:T(8,128)S(1)} %copy.27), kind=kLoop, calls=%fused_computation.275 | loop fusion | flops 343872 | bytes 298496 | tf_op jit(solution)/shard_map/reduce_sum | solution.py:144
  65.0 2.5 %all-reduce.2 = (f32[96]{0:T(128)S(1)}, f32[96]{0:T(128)S(1)}) all-reduce(f32[96]{0:T(128)S(1)} %get-tuple-element.5, f32[96]{0:T(128)S(1)} %get-tuple-element.4), channel_id=1, replica_groups=mesh['groups'=2,'rows'=8,'chan'=2] {'chan'}, use_global_device_ids=true, to_apply=%region_9.10 | all-reduce | flops 192 | bytes 1536 | tf_op jit(solution)/shard_map/psum | solution.py:144
  67.5 1.0 multiply_convert_fusion.2
  68.6 1.3 %collective-permute-start.3 = (bf16[3,32,512]{2,0,1:T(4,128)(2,1)S(1)}, bf16[3,32,512]{2,0,1:T(4,128)(2,1)S(1)}, u32[]{:S(2)}, u32[]{:S(2)}) collective-permute-start(bf16[3,32,512]{2,0,1:T(4,128)(2,1)S(1)} %copy.30), channel_id=1, source_target_pairs={{2,0},{4,2},{6,4},{8,6},{10,8},{12,10},{14,12},{3,1},{5,3},{7,5},{... | collective-permute-start | bytes 294920 | tf_op jit(solution)/shard_map/ppermute | solution.py:20
  69.9 4.6 %collective-permute-start.2 = (bf16[3,32,512]{2,0,1:T(4,128)(2,1)S(1)}, bf16[3,32,512]{2,0,1:T(4,128)(2,1)S(1)}, u32[]{:S(2)}, u32[]{:S(2)}) collective-permute-start(bf16[3,32,512]{2,0,1:T(4,128)(2,1)S(1)} %copy.30), channel_id=1, source_target_pairs={{0,2},{2,4},{4,6},{6,8},{8,10},{10,12},{12,14},{1,3},{3,5},{5,7},{... | collective-permute-start | bytes 294920 | tf_op jit(solution)/shard_map/ppermute | solution.py:18
  74.5 3.8 %fusion.13 = f32[96,1024]{1,0:T(8,128)} fusion(bf16[2048,1024]{1,0:T(8,128)(2,1)} %param.25, f32[96,2048]{1,0:T(8,128)S(1)} %get-tuple-element.69), kind=kOutput, calls=%fused_computation.64 | convolution fusion | flops 404422656 | bytes 5373952 | tf_op jit(solution)/shard_map/dot_general | solution.py:121
  79.9 5.3 %add_add_fusion = f32[3,32,512]{2,0,1:T(4,128)} fusion(f32[9,32,512]{2,0,1:T(8,128)S(1)} %maximum_convert_fusion, f32[3,512]{1,0:T(4,128)S(1)} %fusion.165, f32[3]{0:T(128)} %get-tuple-element.67, f32[512]{0:T(512)S(1)} %bitcast.114, f32[512]{0:T(512)S(1)} %bitcast.112, f32[512]{0:T(512)S(1)} %bitcast.110, f32[512]{0:T(512)S(1)} %bitcast.108, ...), kind=kLoop, calls=%fused_computation.266 | loop fusion | flops 5111808 | bytes 3188808 | tf_op jit(solution)/shard_map/add | solution.py:150
  85.2 5.9 %all-to-all-start.1 = ((f32[3,32,512]{2,0,1:T(4,128)}), f32[3,32,512]{2,0,1:T(4,128)S(1)}, u32[]{:S(2)}, u32[]{:S(2)}) async-start(f32[3,32,512]{2,0,1:T(4,128)} %add_add_fusion), calls=%async_computation.3 | async-start | bytes 524288 | tf_op jit(solution)/shard_map/all_to_all | solution.py:222
  92.1 1.6 %fusion.161 = bf16[96,512]{1,0:T(8,128)(2,1)} fusion(f32[3,32,512]{2,1,0:T(8,128)S(1)} %copy.26, f32[96,512]{1,0:T(8,128)} %reduce-scatter.3.cloned.1.call-done, f32[512]{0:T(512)S(1)} %convert_element_type.107, f32[512]{0:T(512)S(1)} %dynamic_slice.6), kind=kLoop, calls=%fused_computation.271 | loop fusion | flops 196608 | bytes 495616 | tf_op jit(solution)/shard_map/convert_element_type | solution.py:129
  93.7 6.3 %all-to-all-done.1 = f32[3,32,512]{2,0,1:T(4,128)S(1)} async-done(((f32[3,32,512]{2,0,1:T(4,128)}), f32[3,32,512]{2,0,1:T(4,128)S(1)}, u32[]{:S(2)}, u32[]{:S(2)}) %all-to-all-start.1) | async-done | bytes 196640 | tf_op jit(solution)/shard_map/all_to_all | solution.py:222
  99.9 0.8 copy.33
  (198 shorter events, 4.7 us)
Async XLA Ops:
  7.2 20.8 %all-to-all-start = ((bf16[24,4,512]{2,1,0:T(4,128)(2,1)}), bf16[24,4,512]{2,1,0:T(4,128)(2,1)S(1)}, u32[]{:S(2)}, u32[]{:S(2)}) async-start(bf16[24,4,512]{2,1,0:T(4,128)(2,1)} %param.14), calls=%async_computation | async-start | bytes 196608 | tf_op jit(solution)/shard_map/all_to_all | solution.py:188
  14.7 49.3 %reduce-scatter.5.cloned.1.call-start = ((), (), s32[]{:S(2)}) async-start(), calls=%async_computation.5 | async-start | bytes 294912 | tf_op jit(solution)/shard_map/reduce_scatter | solution.py:140
  15.7 22.5 %copy-start.2 = (f32[1,1,512]{2,1,0:T(1,128)}, f32[1,1,512]{2,1,0:T(1,128)S(1)}, u32[]{:S(2)}) copy-start(f32[1,1,512]{2,1,0:T(1,128)S(1)} %get-tuple-element.51) | copy-start | bytes 6148
  15.7 22.5 %copy-start.4 = (f32[1,1,512]{2,1,0:T(1,128)}, f32[1,1,512]{2,1,0:T(1,128)S(1)}, u32[]{:S(2)}) copy-start(f32[1,1,512]{2,1,0:T(1,128)S(1)} %get-tuple-element.52) | copy-start | bytes 6148
  15.7 22.5 %copy-start.6 = (f32[1,1,512]{2,1,0:T(1,128)}, f32[1,1,512]{2,1,0:T(1,128)S(1)}, u32[]{:S(2)}) copy-start(f32[1,1,512]{2,1,0:T(1,128)S(1)} %get-tuple-element.53) | copy-start | bytes 6148
  15.7 22.5 %copy-start.8 = (f32[1,1,512]{2,1,0:T(1,128)}, f32[1,1,512]{2,1,0:T(1,128)S(1)}, u32[]{:S(2)}) copy-start(f32[1,1,512]{2,1,0:T(1,128)S(1)} %get-tuple-element.54) | copy-start | bytes 6148
  15.7 22.5 %copy-start.10 = (f32[1,1,512]{2,1,0:T(1,128)}, f32[1,1,512]{2,1,0:T(1,128)S(1)}, u32[]{:S(2)}) copy-start(f32[1,1,512]{2,1,0:T(1,128)S(1)} %get-tuple-element.55) | copy-start | bytes 6148
  15.7 22.5 %copy-start.12 = (f32[1,1,512]{2,1,0:T(1,128)}, f32[1,1,512]{2,1,0:T(1,128)S(1)}, u32[]{:S(2)}) copy-start(f32[1,1,512]{2,1,0:T(1,128)S(1)} %get-tuple-element.56) | copy-start | bytes 6148
  15.7 22.5 %copy-start.14 = (f32[1,1,512]{2,1,0:T(1,128)}, f32[1,1,512]{2,1,0:T(1,128)S(1)}, u32[]{:S(2)}) copy-start(f32[1,1,512]{2,1,0:T(1,128)S(1)} %get-tuple-element.57) | copy-start | bytes 6148
  15.8 22.5 %copy-start.16 = (f32[1,1,512]{2,1,0:T(1,128)}, f32[1,1,512]{2,1,0:T(1,128)S(1)}, u32[]{:S(2)}) copy-start(f32[1,1,512]{2,1,0:T(1,128)S(1)} %get-tuple-element.58) | copy-start | bytes 6148
  15.8 22.5 %copy-start.18 = (f32[1,1,512]{2,1,0:T(1,128)}, f32[1,1,512]{2,1,0:T(1,128)S(1)}, u32[]{:S(2)}) copy-start(f32[1,1,512]{2,1,0:T(1,128)S(1)} %get-tuple-element.59) | copy-start | bytes 6148
  16.9 21.3 %copy-start.20 = (f32[1,1,512]{2,1,0:T(1,128)}, f32[1,1,512]{2,1,0:T(1,128)S(1)}, u32[]{:S(2)}) copy-start(f32[1,1,512]{2,1,0:T(1,128)S(1)} %get-tuple-element.30) | copy-start | bytes 6148
  16.9 21.3 %copy-start.22 = (f32[1,1,512]{2,1,0:T(1,128)}, f32[1,1,512]{2,1,0:T(1,128)S(1)}, u32[]{:S(2)}) copy-start(f32[1,1,512]{2,1,0:T(1,128)S(1)} %get-tuple-element.31) | copy-start | bytes 6148
  16.9 21.3 %copy-start.24 = (f32[1,1,512]{2,1,0:T(1,128)}, f32[1,1,512]{2,1,0:T(1,128)S(1)}, u32[]{:S(2)}) copy-start(f32[1,1,512]{2,1,0:T(1,128)S(1)} %get-tuple-element.32) | copy-start | bytes 6148
  16.9 21.3 %copy-start.26 = (f32[1,1,512]{2,1,0:T(1,128)}, f32[1,1,512]{2,1,0:T(1,128)S(1)}, u32[]{:S(2)}) copy-start(f32[1,1,512]{2,1,0:T(1,128)S(1)} %get-tuple-element.33) | copy-start | bytes 6148
  17.0 21.3 %copy-start.28 = (f32[1,1,512]{2,1,0:T(1,128)}, f32[1,1,512]{2,1,0:T(1,128)S(1)}, u32[]{:S(2)}) copy-start(f32[1,1,512]{2,1,0:T(1,128)S(1)} %get-tuple-element.34) | copy-start | bytes 6148
  17.0 21.3 %copy-start.30 = (f32[1,1,512]{2,1,0:T(1,128)}, f32[1,1,512]{2,1,0:T(1,128)S(1)}, u32[]{:S(2)}) copy-start(f32[1,1,512]{2,1,0:T(1,128)S(1)} %get-tuple-element.35) | copy-start | bytes 6148
  17.0 21.3 %copy-start.32 = (f32[1,1,512]{2,1,0:T(1,128)}, f32[1,1,512]{2,1,0:T(1,128)S(1)}, u32[]{:S(2)}) copy-start(f32[1,1,512]{2,1,0:T(1,128)S(1)} %get-tuple-element.36) | copy-start | bytes 6148
  17.0 21.3 %copy-start.34 = (f32[1,1,512]{2,1,0:T(1,128)}, f32[1,1,512]{2,1,0:T(1,128)S(1)}, u32[]{:S(2)}) copy-start(f32[1,1,512]{2,1,0:T(1,128)S(1)} %get-tuple-element.37) | copy-start | bytes 6148
  17.0 21.3 %copy-start.36 = (f32[1,1,512]{2,1,0:T(1,128)}, f32[1,1,512]{2,1,0:T(1,128)S(1)}, u32[]{:S(2)}) copy-start(f32[1,1,512]{2,1,0:T(1,128)S(1)} %get-tuple-element.38) | copy-start | bytes 6148
  17.0 21.3 %copy-start.38 = (f32[1,1,512]{2,1,0:T(1,128)}, f32[1,1,512]{2,1,0:T(1,128)S(1)}, u32[]{:S(2)}) copy-start(f32[1,1,512]{2,1,0:T(1,128)S(1)} %get-tuple-element.39) | copy-start | bytes 6148
  17.0 21.3 %copy-start.40 = (f32[1,1,512]{2,1,0:T(1,128)}, f32[1,1,512]{2,1,0:T(1,128)S(1)}, u32[]{:S(2)}) copy-start(f32[1,1,512]{2,1,0:T(1,128)S(1)} %get-tuple-element.40) | copy-start | bytes 6148
  17.0 21.3 %copy-start.42 = (f32[1,1,512]{2,1,0:T(1,128)}, f32[1,1,512]{2,1,0:T(1,128)S(1)}, u32[]{:S(2)}) copy-start(f32[1,1,512]{2,1,0:T(1,128)S(1)} %get-tuple-element.41) | copy-start | bytes 6148
  17.0 21.3 %copy-start.44 = (f32[1,1,512]{2,1,0:T(1,128)}, f32[1,1,512]{2,1,0:T(1,128)S(1)}, u32[]{:S(2)}) copy-start(f32[1,1,512]{2,1,0:T(1,128)S(1)} %get-tuple-element.42) | copy-start | bytes 6148
  17.0 21.3 %copy-start.46 = (f32[1,1,512]{2,1,0:T(1,128)}, f32[1,1,512]{2,1,0:T(1,128)S(1)}, u32[]{:S(2)}) copy-start(f32[1,1,512]{2,1,0:T(1,128)S(1)} %get-tuple-element.43) | copy-start | bytes 6148
  17.1 21.3 %copy-start.48 = (f32[1,1,512]{2,1,0:T(1,128)}, f32[1,1,512]{2,1,0:T(1,128)S(1)}, u32[]{:S(2)}) copy-start(f32[1,1,512]{2,1,0:T(1,128)S(1)} %get-tuple-element.44) | copy-start | bytes 6148
  28.0 6.9 %collective-permute-start.1 = (bf16[3,32,512]{2,0,1:T(4,128)(2,1)S(1)}, bf16[3,32,512]{2,0,1:T(4,128)(2,1)S(1)}, u32[]{:S(2)}, u32[]{:S(2)}) collective-permute-start(bf16[3,32,512]{2,0,1:T(4,128)(2,1)S(1)} %bitcast.86), channel_id=1, source_target_pairs={{2,0},{4,2},{6,4},{8,6},{10,8},{12,10},{14,12},{3,1},{5,3},{7,5},{... | collective-permute-start | bytes 294920 | tf_op jit(solution)/shard_map/ppermute | solution.py:20
  29.3 8.5 %collective-permute-start = (bf16[3,32,512]{2,0,1:T(4,128)(2,1)S(1)}, bf16[3,32,512]{2,0,1:T(4,128)(2,1)S(1)}, u32[]{:S(2)}, u32[]{:S(2)}) collective-permute-start(bf16[3,32,512]{2,0,1:T(4,128)(2,1)S(1)} %bitcast.87), channel_id=1, source_target_pairs={{0,2},{2,4},{4,6},{6,8},{8,10},{10,12},{12,14},{1,3},{3,5},{5,7},{... | collective-permute-start | bytes 294920 | tf_op jit(solution)/shard_map/ppermute | solution.py:18
  54.3 37.8 %reduce-scatter.3.cloned.1.call-start = ((), (), s32[]{:S(2)}) async-start(), calls=%async_computation.4 | async-start | bytes 589824 | tf_op jit(solution)/shard_map/reduce_scatter | solution.py:120
  68.6 10.1 %collective-permute-start.3 = (bf16[3,32,512]{2,0,1:T(4,128)(2,1)S(1)}, bf16[3,32,512]{2,0,1:T(4,128)(2,1)S(1)}, u32[]{:S(2)}, u32[]{:S(2)}) collective-permute-start(bf16[3,32,512]{2,0,1:T(4,128)(2,1)S(1)} %copy.30), channel_id=1, source_target_pairs={{2,0},{4,2},{6,4},{8,6},{10,8},{12,10},{14,12},{3,1},{5,3},{7,5},{... | collective-permute-start | bytes 294920 | tf_op jit(solution)/shard_map/ppermute | solution.py:20
  69.9 9.3 %collective-permute-start.2 = (bf16[3,32,512]{2,0,1:T(4,128)(2,1)S(1)}, bf16[3,32,512]{2,0,1:T(4,128)(2,1)S(1)}, u32[]{:S(2)}, u32[]{:S(2)}) collective-permute-start(bf16[3,32,512]{2,0,1:T(4,128)(2,1)S(1)} %copy.30), channel_id=1, source_target_pairs={{0,2},{2,4},{4,6},{6,8},{8,10},{10,12},{12,14},{1,3},{3,5},{5,7},{... | collective-permute-start | bytes 294920 | tf_op jit(solution)/shard_map/ppermute | solution.py:18
  85.2 14.7 %all-to-all-start.1 = ((f32[3,32,512]{2,0,1:T(4,128)}), f32[3,32,512]{2,0,1:T(4,128)S(1)}, u32[]{:S(2)}, u32[]{:S(2)}) async-start(f32[3,32,512]{2,0,1:T(4,128)} %add_add_fusion), calls=%async_computation.3 | async-start | bytes 524288 | tf_op jit(solution)/shard_map/all_to_all | solution.py:222
  (59 other events, 411.7 us)
Sparse Core Ops, SparseCore 0:
  54.4 9.4 reduce-scatter.4
  78.8 8.9 reduce-scatter.2
where the time goes:
time: 109 us; the launch traced here: 108 us
  starting transfers between devices  25.1 us (23%)
  waiting for transfers between devices  20.2 us (19%)
  other arithmetic  19.8 us (18%)
  between operations  15.5 us (14%)
  matrix products  14.5 us (13%)
  blocking collectives  6.89 us (6%)
  local copies, waits for them, and re-layouts  5.62 us (5%)
    reduce_scatter x1, waiting for transfers between devices, local_block(): lax.psum_scatter(grad_terms.astype(jnp.bfloat16), 'chan', scatter_dimensi...  9.45 us
    ppermute x2, starting transfers between devices, with_halo(): lax.ppermute(tail, axis, [(i, (i + 1) % count) for i in range(ends)])  9.11 us
    all_to_all x1, starting transfers between devices, per_device(): lax.all_to_all(latents, 'rows', split_axis=0, concat_axis=1, tiled=True)  7.45 us
    all_to_all x1, waiting for transfers between devices, per_device(): lax.all_to_all(gradient, 'rows', split_axis=1, concat_axis=0, tiled=True)  6.28 us
    all_to_all x1, starting transfers between devices, per_device(): lax.all_to_all(gradient, 'rows', split_axis=1, concat_axis=0, tiled=True)  5.88 us
    add x1, other arithmetic, local_block(): stencil(grad_pad, kernel[::-1, ::-1], masks) + class_tokens[:, None, :]  5.34 us
    reduce_sum x1, other arithmetic, local_block(): jnp.sum(flat, 1)  5.05 us
    dot_general x1, matrix products, local_block(): jnp.dot(active, down_weight, preferred_element_type=jnp.float32)  3.82 us
  transfers between devices with their start and end apart: 8, of which 5 were waited for; matrix products, arithmetic and copies ran while one was open for 23% of the time, Pallas kernels for 0%

commit v1 on v0

--- a/solution.py
+++ b/solution.py
@@ -5,6 +5,18 @@
 
 KAPPA = 0.7978845608028654
 EPSILON = 1e-06
+
+
+def lead_sections_on_mesh(a0, chip_axis):
+    return jnp.concatenate(
+        lax.all_to_all(
+            jnp.stack(jnp.split(a0, lax.axis_size(chip_axis), 0), 0),
+            axis_name=chip_axis,
+            split_axis=0,
+            concat_axis=0,
+        ),
+        axis=1,
+    )
 
 
 def with_halo(cells, sides, width):
@@ -185,7 +197,7 @@
     slope_image = lax.dot_general(
         direction, down_weight, (((1,), (1,)), ((), ())), preferred_element_type=jnp.float32
     )
-    latent_rows = lax.all_to_all(latents, "rows", split_axis=0, concat_axis=1, tiled=True)
+    latent_rows = lead_sections_on_mesh(latents, chip_axis="rows")
     height = latent_rows.shape[0]
     width = latent_rows.shape[1]
     row_first = lax.axis_index("rows") * height

time: 109 us -> 109 us (level)
  local copies, waits for them, and re-layouts: 5.62 us -> 15.9 us
  other arithmetic: 19.8 us -> 10.7 us
  between operations: 15.5 us -> 14.2 us
    unnamed x166 -> x15, local copies, waits for them, and re-layouts: 0.36 us -> 9.3 us
    add x1, other arithmetic: 5.34 us -> 1.19 us  [local_block(): stencil(grad_pad, kernel[::-1, ::-1], masks) + class_tokens[:, None, :]]
    reduce_sum x1, other arithmetic: 5.05 us -> 1.85 us  [local_block(): jnp.sum(flat, 1)]
    reduce_scatter x1, waiting for transfers between devices: 9.45 us -> 6.76 us  [local_block(): lax.psum_scatter(grad_terms.astype(jnp.bfloat16), 'chan', scatter_dimensi...]
    another operation x0 -> x1, local copies, waits for them, and re-layouts: none -> 1.31 us  [lead_sections_on_mesh(): jnp.stack(jnp.split(a0, lax.axis_size(chip_axis), 0), 0)]
  transfers between devices with their start and end apart: 8 -> 8, of which waited for: 5 -> 6; matrix products, arithmetic and copies ran while one was open for 23% -> 21% of each run, Pallas kernels for 0% -> 0%
where the time goes in v1:
time: 109 us; the launch traced here: 108 us
  starting transfers between devices  25.7 us (24%)
  waiting for transfers between devices  19.2 us (18%)
  local copies, waits for them, and re-layouts  15.9 us (15%)
  matrix products  15.1 us (14%)
  between operations  14.2 us (13%)
  other arithmetic  10.7 us (10%)
  blocking collectives  7 us (6%)
    unnamed x15, local copies, waits for them, and re-layouts  9.3 us
    ppermute x2, starting transfers between devices, with_halo(): lax.ppermute(tail, axis, [(i, (i + 1) % count) for i in range(ends)])  9.1 us
    all_to_all x1, starting transfers between devices, lead_sections_on_mesh(): lax.all_to_all(jnp.stack(jnp.split(a0, lax.axis_size(chip_axis), 0), 0),...  7.31 us
    reduce_scatter x1, waiting for transfers between devices, local_block(): lax.psum_scatter(grad_terms.astype(jnp.bfloat16), 'chan', scatter_dimensi...  6.76 us
    all_to_all x1, waiting for transfers between devices, per_device(): lax.all_to_all(gradient, 'rows', split_axis=1, concat_axis=0, tiled=True)  6.69 us
    all_to_all x1, starting transfers between devices, per_device(): lax.all_to_all(gradient, 'rows', split_axis=1, concat_axis=0, tiled=True)  6.58 us
    ppermute x2, waiting for transfers between devices, with_halo(): lax.ppermute(tail, axis, [(i, (i + 1) % count) for i in range(ends)])  4.13 us
    dot_general x1, matrix products, local_block(): jnp.dot(active, down_weight, preferred_element_type=jnp.float32)  3.81 us
  transfers between devices with their start and end apart: 8, of which 6 were waited for; matrix products, arithmetic and copies ran while one was open for 21% of the time, Pallas kernels for 0%

profile of v1, /device:TPU:0, one launch (start us, length us, event | category | flops | bytes accessed | tf_op | source)
XLA Modules:
  0.0 107.8 jit_solution(15557042042113184184)
XLA Ops:
  7.2 1.4 %constant_dynamic-update-slice_fusion.7 = bf16[8,3,4,512]{3,2,1,0:T(4,128)(2,1)} fusion(bf16[24,4,512]{2,1,0:T(4,128)(2,1)} %param.14), kind=kLoop, calls=%fused_computation.293 | loop fusion | bytes 24576
  8.6 1.3 %constant_dynamic-update-slice_fusion.6 = bf16[8,3,4,512]{3,2,1,0:T(4,128)(2,1)} fusion(bf16[8,3,4,512]{3,2,1,0:T(4,128)(2,1)} %constant_dynamic-update-slice_fusion.7, bf16[24,4,512]{2,1,0:T(4,128)(2,1)} %param.14), kind=kLoop, calls=%fused_computation.292 | loop fusion | bytes 24576
  9.9 1.3 %constant_dynamic-update-slice_fusion.5 = bf16[8,3,4,512]{3,2,1,0:T(4,128)(2,1)} fusion(bf16[8,3,4,512]{3,2,1,0:T(4,128)(2,1)} %constant_dynamic-update-slice_fusion.6, bf16[24,4,512]{2,1,0:T(4,128)(2,1)} %param.14), kind=kLoop, calls=%fused_computation.291 | loop fusion | bytes 24576
  11.2 1.3 %constant_dynamic-update-slice_fusion.4 = bf16[8,3,4,512]{3,2,1,0:T(4,128)(2,1)} fusion(bf16[8,3,4,512]{3,2,1,0:T(4,128)(2,1)} %constant_dynamic-update-slice_fusion.5, bf16[24,4,512]{2,1,0:T(4,128)(2,1)} %param.14), kind=kLoop, calls=%fused_computation.290 | loop fusion | bytes 24576
  12.5 1.3 %constant_dynamic-update-slice_fusion.3 = bf16[8,3,4,512]{3,2,1,0:T(4,128)(2,1)} fusion(bf16[8,3,4,512]{3,2,1,0:T(4,128)(2,1)} %constant_dynamic-update-slice_fusion.4, bf16[24,4,512]{2,1,0:T(4,128)(2,1)} %param.14), kind=kLoop, calls=%fused_computation.289 | loop fusion | bytes 24576
  13.8 1.3 %constant_dynamic-update-slice_fusion.2 = bf16[8,3,4,512]{3,2,1,0:T(4,128)(2,1)} fusion(bf16[8,3,4,512]{3,2,1,0:T(4,128)(2,1)} %constant_dynamic-update-slice_fusion.3, bf16[24,4,512]{2,1,0:T(4,128)(2,1)} %param.14), kind=kLoop, calls=%fused_computation.288 | loop fusion | bytes 24576
  15.1 1.3 %constant_dynamic-update-slice_fusion.1 = bf16[8,3,4,512]{3,2,1,0:T(4,128)(2,1)} fusion(bf16[8,3,4,512]{3,2,1,0:T(4,128)(2,1)} %constant_dynamic-update-slice_fusion.2, bf16[24,4,512]{2,1,0:T(4,128)(2,1)} %param.14), kind=kLoop, calls=%fused_computation.287 | loop fusion | bytes 24576
  16.5 1.3 %constant_dynamic-update-slice_fusion = bf16[8,3,4,512]{3,2,1,0:T(4,128)(2,1)} fusion(bf16[8,3,4,512]{3,2,1,0:T(4,128)(2,1)} %constant_dynamic-update-slice_fusion.1, bf16[24,4,512]{2,1,0:T(4,128)(2,1)} %param.14), kind=kLoop, calls=%fused_computation.286 | loop fusion | bytes 24576 | tf_op jit(solution)/shard_map/stack | solution.py:13
  17.8 7.3 %all-to-all-start = ((bf16[8,3,4,512]{3,2,1,0:T(4,128)(2,1)}), bf16[8,3,4,512]{3,2,1,0:T(4,128)(2,1)S(1)}, u32[]{:S(2)}, u32[]{:S(2)}) async-start(bf16[8,3,4,512]{3,2,1,0:T(4,128)(2,1)} %constant_dynamic-update-slice_fusion), calls=%async_computation | async-start | bytes 196608 | tf_op jit(solution)/shard_map/all_to_all | solution.py:12
  25.1 1.1 %fusion.194 = (f32[1,1,512]{2,1,0:T(1,128)S(1)}, f32[1,1,512]{2,1,0:T(1,128)S(1)}, f32[1,1,512]{2,1,0:T(1,128)S(1)}, f32[1,1,512]{2,1,0:T(1,128)S(1)}, f32[1,1,5...) fusion(bf16[7,7,512]{2,1,0:T(8,128)(2,1)} %param.19), kind=kLoop, calls=%fused_computation.332 | loop fusion | bytes 45056 | tf_op jit(solution)/shard_map/slice | solution.py:61
  26.3 1.1 %fusion.193 = (f32[1,1,512]{2,1,0:T(1,128)S(1)}, f32[1,1,512]{2,1,0:T(1,128)S(1)}, f32[1,1,512]{2,1,0:T(1,128)S(1)}, f32[1,1,512]{2,1,0:T(1,128)S(1)}, f32[1,1,5...) fusion(bf16[7,7,512]{2,1,0:T(8,128)(2,1)} %param.19), kind=kLoop, calls=%fused_computation.331 | loop fusion | bytes 77824 | tf_op jit(solution)/shard_map/slice | solution.py:61
  27.4 1.0 fusion.192
  34.1 3.4 %fusion.174 = f32[3,2048]{1,0:T(4,128)S(1)} fusion(bf16[2048,1024]{1,0:T(8,128)(2,1)} %param.25, f32[3,1024]{1,0:T(4,128)S(1)} %fusion.179, f32[1024]{0:T(1024)S(1)} %convert_element_type.93), kind=kOutput, calls=%fused_computation.297 | convolution fusion | flops 12589056 | bytes 4235264 | tf_op jit(solution)/shard_map/dot_general | solution.py:197
  37.8 1.3 %collective-permute-start.1 = (bf16[3,32,512]{2,1,0:T(8,128)(2,1)S(1)}, bf16[3,32,512]{2,1,0:T(8,128)(2,1)S(1)}, u32[]{:S(2)}, u32[]{:S(2)}) collective-permute-start(bf16[3,32,512]{2,1,0:T(8,128)(2,1)S(1)} %reshape.77), channel_id=1, source_target_pairs={{2,0},{4,2},{6,4},{8,6},{10,8},{12,10},{14,12},{3,1},{5,3},{7,5},{... | collective-permute-start | bytes 294920 | tf_op jit(solution)/shard_map/ppermute | solution.py:32
  39.1 4.6 %collective-permute-start = (bf16[3,32,512]{2,1,0:T(8,128)(2,1)S(1)}, bf16[3,32,512]{2,1,0:T(8,128)(2,1)S(1)}, u32[]{:S(2)}, u32[]{:S(2)}) collective-permute-start(bf16[3,32,512]{2,1,0:T(8,128)(2,1)S(1)} %reshape.77), channel_id=1, source_target_pairs={{0,2},{2,4},{4,6},{6,8},{8,10},{10,12},{12,14},{1,3},{3,5},{5,7},{... | collective-permute-start | bytes 294920 | tf_op jit(solution)/shard_map/ppermute | solution.py:30
  44.3 1.9 %collective-permute-done = bf16[3,32,512]{2,1,0:T(8,128)(2,1)S(1)} collective-permute-done((bf16[3,32,512]{2,1,0:T(8,128)(2,1)S(1)}, bf16[3,32,512]{2,1,0:T(8,128)(2,1)S(1)}, u32[]{:S(2)}, u32[]{:S(2)}) %collective-permute-start) | collective-permute-done | bytes 98336 | tf_op jit(solution)/shard_map/ppermute | solution.py:30
  46.3 1.8 %fusion.190 = (f32[3,32]{1,0:T(4,128)S(1)}, f32[3,32]{1,0:T(4,128)S(1)}, f32[3,32,512]{2,1,0:T(8,128)S(1)}) fusion(f32[512]{0:T(512)S(1)} %convert_element_type.101, f32[3]{0:T(128)S(1)} %get-tuple-element.67, f32[512]{0:T(512)S(1)} %bitcast.125, f32[9,38,512]{2,1,0:T(8,128)S(1)} %multiply_add_fusion.1, f32[512]{0:T(512)S(1)} %bitcast.123, ...), kind=kLoop, calls=%fused_computation.329 | loop fusion | flops 5259072 | bytes 9933640 | tf_op jit(solution)/shard_map/reduce_sum | solution.py:118
  48.4 2.5 %all-reduce.3 = (f32[96]{0:T(128)S(1)}, f32[96]{0:T(128)S(1)}) all-reduce(f32[96]{0:T(128)S(1)} %reduce_sum.43, f32[96]{0:T(128)S(1)} %reduce_sum.41), channel_id=1, replica_groups=mesh['groups'=2,'rows'=8,'chan'=2] {'chan'}, use_global_device_ids=true, to_apply=%region_3.4 | all-reduce | flops 192 | bytes 1536 | tf_op jit(solution)/shard_map/psum | solution.py:118
  50.9 2.1 %all_gather.3 = bf16[96,1024]{1,0:T(8,128)(2,1)S(1)} all-gather(bf16[96,512]{1,0:T(8,128)(2,1)S(1)} %add_convert_fusion), channel_id=1, replica_groups=mesh['groups'=2,'rows'=8,'chan'=2] {'chan'}, dimensions={1}, use_global_device_ids=true | all-gather | bytes 294912 | tf_op jit(solution)/shard_map/all_gather | solution.py:126
  53.0 3.4 %fusion.6 = (bf16[96,2048]{1,0:T(8,128)(2,1)S(1)}, f32[96,2048]{1,0:T(8,128)S(1)}) fusion(f32[3,2048]{1,0:T(4,128)S(1)} %fusion.181, f32[2048]{0:T(1024)S(1)} %convert_element_type.105, bf16[96,1024]{1,0:T(8,128)(2,1)S(1)} %all_gather.3, bf16[1024,2048]{1,0:T(8,128)(2,1)} %param.23), kind=kOutput, calls=%fused_computation.54 | convolution fusion | flops 406585344 | bytes 5603328 | tf_op jit(solution)/shard_map/dot_general | solution.py:125
  56.5 2.1 %convolution_convert_fusion = bf16[96,1024]{1,0:T(8,128)(2,1)} fusion(bf16[96,2048]{1,0:T(8,128)(2,1)S(1)} %get-tuple-element.68, bf16[1024,2048]{1,0:T(8,128)(2,1)S(1)} %copy-done.1), kind=kOutput, calls=%fused_computation.45 | convolution fusion | flops 402751488 | bytes 4784128 | tf_op jit(solution)/shard_map/dot_general | solution.py:149
  58.7 3.8 %fusion.11 = f32[96,1024]{1,0:T(8,128)} fusion(bf16[2048,1024]{1,0:T(8,128)(2,1)} %param.25, f32[96,2048]{1,0:T(8,128)S(1)} %get-tuple-element.69), kind=kOutput, calls=%fused_computation.61 | convolution fusion | flops 404422656 | bytes 5373952 | tf_op jit(solution)/shard_map/dot_general | solution.py:133
  62.5 6.8 %reduce-scatter.5.cloned.1.call-done = bf16[96,512]{1,0:T(8,128)(2,1)} async-done(((bf16[96,1024]{1,0:T(8,128)(2,1)}), bf16[96,512]{1,0:T(8,128)(2,1)}) %reduce-scatter.5.cloned.1.call-update) | async-done | bytes 98320 | tf_op jit(solution)/shard_map/reduce_scatter | solution.py:152
  69.3 1.1 %fusion.171 = (f32[96]{0:T(128)S(1)}, f32[96]{0:T(128)S(1)}) fusion(bf16[96,512]{1,0:T(8,128)(2,1)} %reduce-scatter.5.cloned.1.call-done, f32[512]{0:T(512)S(1)} %convert_element_type.102, f32[96]{0:T(128)S(1)} %get-tuple-element.61, f32[96]{0:T(128)S(1)} %get-tuple-element.60, f32[3,32,512]{2,1,0:T(8,128)S(1)} %get-tuple-element.10), kind=kLoop, calls=%fused_computation.282 | loop fusion | flops 343872 | bytes 298496 | tf_op jit(solution)/shard_map/reduce_sum | solution.py:156
  70.4 2.5 %all-reduce.2 = (f32[96]{0:T(128)S(1)}, f32[96]{0:T(128)S(1)}) all-reduce(f32[96]{0:T(128)S(1)} %get-tuple-element.5, f32[96]{0:T(128)S(1)} %get-tuple-element.4), channel_id=1, replica_groups=mesh['groups'=2,'rows'=8,'chan'=2] {'chan'}, use_global_device_ids=true, to_apply=%region_9.10 | all-reduce | flops 192 | bytes 1536 | tf_op jit(solution)/shard_map/psum | solution.py:156
  73.9 1.3 %collective-permute-start.3 = (bf16[3,32,512]{2,1,0:T(8,128)(2,1)S(1)}, bf16[3,32,512]{2,1,0:T(8,128)(2,1)S(1)}, u32[]{:S(2)}, u32[]{:S(2)}) collective-permute-start(bf16[3,32,512]{2,1,0:T(8,128)(2,1)S(1)} %bitcast.100), channel_id=1, source_target_pairs={{2,0},{4,2},{6,4},{8,6},{10,8},{12,10},{14,12},{3,1},{5,3},{7,5},{... | collective-permute-start | bytes 294920 | tf_op jit(solution)/shard_map/ppermute | solution.py:32
  75.2 4.6 %collective-permute-start.2 = (bf16[3,32,512]{2,1,0:T(8,128)(2,1)S(1)}, bf16[3,32,512]{2,1,0:T(8,128)(2,1)S(1)}, u32[]{:S(2)}, u32[]{:S(2)}) collective-permute-start(bf16[3,32,512]{2,1,0:T(8,128)(2,1)S(1)} %bitcast.101), channel_id=1, source_target_pairs={{0,2},{2,4},{4,6},{6,8},{8,10},{10,12},{12,14},{1,3},{3,5},{5,7},{... | collective-permute-start | bytes 294920 | tf_op jit(solution)/shard_map/ppermute | solution.py:30
  80.8 2.3 %collective-permute-done.2 = bf16[3,32,512]{2,1,0:T(8,128)(2,1)S(1)} collective-permute-done((bf16[3,32,512]{2,1,0:T(8,128)(2,1)S(1)}, bf16[3,32,512]{2,1,0:T(8,128)(2,1)S(1)}, u32[]{:S(2)}, u32[]{:S(2)}) %collective-permute-start.2) | collective-permute-done | bytes 98336 | tf_op jit(solution)/shard_map/ppermute | solution.py:30
  83.1 1.2 %fusion.172 = f32[3,32,512]{2,1,0:T(8,128)S(1)} fusion(f32[9,32,512]{2,1,0:T(8,128)S(1)} %maximum_convert_fusion, f32[3,512]{1,0:T(4,128)S(1)} %fusion.175, f32[3]{0:T(128)S(1)} %get-tuple-element.67, f32[512]{0:T(512)S(1)} %bitcast.126, f32[512]{0:T(512)S(1)} %bitcast.124, f32[512]{0:T(512)S(1)} %bitcast.122, f32[512]{0:T(512)S(1)} %bitcast.120, ...), kind=kLoop, calls=%fused_computation.285 | loop fusion | flops 5111808 | bytes 2274304 | tf_op jit(solution)/shard_map/add | solution.py:162
  85.1 6.6 %all-to-all-start.1 = ((f32[3,32,512]{2,0,1:T(4,128)}), f32[3,32,512]{2,0,1:T(4,128)S(1)}, u32[]{:S(2)}, u32[]{:S(2)}) async-start(f32[3,32,512]{2,0,1:T(4,128)} %copy.20), calls=%async_computation.3 | async-start | bytes 524288 | tf_op jit(solution)/shard_map/all_to_all | solution.py:234
  91.9 1.6 %fusion.170 = bf16[96,512]{1,0:T(8,128)(2,1)} fusion(f32[3,32,512]{2,1,0:T(8,128)S(1)} %slice.733, f32[96,512]{1,0:T(8,128)} %reduce-scatter.3.cloned.1.call-done, f32[512]{0:T(512)S(1)} %convert_element_type.107, f32[512]{0:T(512)S(1)} %dynamic_slice.6), kind=kLoop, calls=%fused_computation.278 | loop fusion | flops 196608 | bytes 495616 | tf_op jit(solution)/shard_map/convert_element_type | solution.py:141
  93.5 6.7 %all-to-all-done.1 = f32[3,32,512]{2,0,1:T(4,128)S(1)} async-done(((f32[3,32,512]{2,0,1:T(4,128)}), f32[3,32,512]{2,0,1:T(4,128)S(1)}, u32[]{:S(2)}, u32[]{:S(2)}) %all-to-all-start.1) | async-done | bytes 196640 | tf_op jit(solution)/shard_map/all_to_all | solution.py:234
  (45 shorter events, 11.0 us)
Async XLA Ops:
  7.2 24.8 %copy-start = (bf16[1000,512]{1,0:T(8,128)(2,1)S(1)}, bf16[1000,512]{1,0:T(8,128)(2,1)}, u32[]{:S(2)}) copy-start(bf16[1000,512]{1,0:T(8,128)(2,1)} %param.17) | copy-start | bytes 3072004
  17.8 19.9 %all-to-all-start = ((bf16[8,3,4,512]{3,2,1,0:T(4,128)(2,1)}), bf16[8,3,4,512]{3,2,1,0:T(4,128)(2,1)S(1)}, u32[]{:S(2)}, u32[]{:S(2)}) async-start(bf16[8,3,4,512]{3,2,1,0:T(4,128)(2,1)} %constant_dynamic-update-slice_fusion), calls=%async_computation | async-start | bytes 196608 | tf_op jit(solution)/shard_map/all_to_all | solution.py:12
  25.1 44.2 %reduce-scatter.5.cloned.1.call-start = ((), (), s32[]{:S(2)}) async-start(), calls=%async_computation.5 | async-start | bytes 294912 | tf_op jit(solution)/shard_map/reduce_scatter | solution.py:152
  37.8 6.5 %collective-permute-start.1 = (bf16[3,32,512]{2,1,0:T(8,128)(2,1)S(1)}, bf16[3,32,512]{2,1,0:T(8,128)(2,1)S(1)}, u32[]{:S(2)}, u32[]{:S(2)}) collective-permute-start(bf16[3,32,512]{2,1,0:T(8,128)(2,1)S(1)} %reshape.77), channel_id=1, source_target_pairs={{2,0},{4,2},{6,4},{8,6},{10,8},{12,10},{14,12},{3,1},{5,3},{7,5},{... | collective-permute-start | bytes 294920 | tf_op jit(solution)/shard_map/ppermute | solution.py:32
  39.1 7.1 %collective-permute-start = (bf16[3,32,512]{2,1,0:T(8,128)(2,1)S(1)}, bf16[3,32,512]{2,1,0:T(8,128)(2,1)S(1)}, u32[]{:S(2)}, u32[]{:S(2)}) collective-permute-start(bf16[3,32,512]{2,1,0:T(8,128)(2,1)S(1)} %reshape.77), channel_id=1, source_target_pairs={{0,2},{2,4},{4,6},{6,8},{8,10},{10,12},{12,14},{1,3},{3,5},{5,7},{... | collective-permute-start | bytes 294920 | tf_op jit(solution)/shard_map/ppermute | solution.py:30
  50.8 5.6 %copy-start.1 = (bf16[1024,2048]{1,0:T(8,128)(2,1)S(1)}, bf16[1024,2048]{1,0:T(8,128)(2,1)}, u32[]{:S(2)}) copy-start(bf16[1024,2048]{1,0:T(8,128)(2,1)} %param.23) | copy-start | bytes 12582916
  58.6 33.3 %reduce-scatter.3.cloned.1.call-start = ((), (), s32[]{:S(2)}) async-start(), calls=%async_computation.4 | async-start | bytes 589824 | tf_op jit(solution)/shard_map/reduce_scatter | solution.py:132
  58.7 33.1 %copy-start.2 = (bf16[1024]{0:T(1024)(128)(2,1)S(1)}, bf16[1024]{0:T(1024)(128)(2,1)}, u32[]{:S(2)}) copy-start(bf16[1024]{0:T(1024)(128)(2,1)} %param.27) | copy-start | bytes 6148
  58.7 33.1 %copy-start.3 = (bf16[512]{0:T(512)(128)(2,1)S(1)}, bf16[512]{0:T(512)(128)(2,1)}, u32[]{:S(2)}) copy-start(bf16[512]{0:T(512)(128)(2,1)} %param.26) | copy-start | bytes 3076
  73.9 6.9 %collective-permute-start.3 = (bf16[3,32,512]{2,1,0:T(8,128)(2,1)S(1)}, bf16[3,32,512]{2,1,0:T(8,128)(2,1)S(1)}, u32[]{:S(2)}, u32[]{:S(2)}) collective-permute-start(bf16[3,32,512]{2,1,0:T(8,128)(2,1)S(1)} %bitcast.100), channel_id=1, source_target_pairs={{2,0},{4,2},{6,4},{8,6},{10,8},{12,10},{14,12},{3,1},{5,3},{7,5},{... | collective-permute-start | bytes 294920 | tf_op jit(solution)/shard_map/ppermute | solution.py:32
  75.2 7.9 %collective-permute-start.2 = (bf16[3,32,512]{2,1,0:T(8,128)(2,1)S(1)}, bf16[3,32,512]{2,1,0:T(8,128)(2,1)S(1)}, u32[]{:S(2)}, u32[]{:S(2)}) collective-permute-start(bf16[3,32,512]{2,1,0:T(8,128)(2,1)S(1)} %bitcast.101), channel_id=1, source_target_pairs={{0,2},{2,4},{4,6},{6,8},{8,10},{10,12},{12,14},{1,3},{3,5},{5,7},{... | collective-permute-start | bytes 294920 | tf_op jit(solution)/shard_map/ppermute | solution.py:30
  85.1 15.0 %all-to-all-start.1 = ((f32[3,32,512]{2,0,1:T(4,128)}), f32[3,32,512]{2,0,1:T(4,128)S(1)}, u32[]{:S(2)}, u32[]{:S(2)}) async-start(f32[3,32,512]{2,0,1:T(4,128)} %copy.20), calls=%async_computation.3 | async-start | bytes 524288 | tf_op jit(solution)/shard_map/all_to_all | solution.py:234
Sparse Core Ops, SparseCore 0:
  58.7 10.5 reduce-scatter.4
  71.5 8.9 reduce-scatter.2
